TPU v7x, 32 devices: a whole 2x2x4 slice. The times are simulated.
32 devices in a mesh: ctx: 8 (over z, x), chan: 4 (over y, core).
Axes of the slice: x: 2, y: 2, z: 4, core: 2. Of those that a mesh axis runs over, the one named last changes fastest.
Arguments:
- query_in: bfloat16 [4096, 1024], P('chan', 'ctx'), may hold values from -6 to 6
- key_in: bfloat16 [4096, 1024], P('chan', 'ctx'), may hold values from -6 to 6
- value_in: bfloat16 [4096, 1024], P('chan', 'ctx'), may hold values from -6 to 6
- short_kernel: float32 [3, 3, 4096], P(None, None, 'chan'), may hold values from -3.5 to 3.5
- filter_in: float32 [64, 64], replicated, may hold values from -0.75 to 0.75
- filter_out: float32 [64, 4096], P(None, 'chan'), may hold values from -0.75 to 0.75
- filter_decay: float32 [4096], P('chan'), may hold values from 0.5 to 40
- skip_gain: float32 [4096], P('chan'), may hold values from -3 to 3
- grad_out: bfloat16 [4096, 1024], P('chan', 'ctx'), may hold values from -6 to 6
Outputs:
- output: bfloat16 [4096, 1024], P('chan', 'ctx')
- grad_query: bfloat16 [4096, 1024], P('chan', 'ctx')
- grad_key: bfloat16 [4096, 1024], P('chan', 'ctx')
- grad_value: bfloat16 [4096, 1024], P('chan', 'ctx')
- grad_short: float32 [3, 3, 4096], P(None, None, 'chan')
- grad_filter_in: float32 [64, 64], replicated
- grad_filter_out: float32 [64, 4096], P(None, 'chan')
- grad_decay: float32 [4096], P('chan')
- grad_skip: float32 [4096], P('chan')
All inputs are finite; a program needn't handle non-finite values.
Results may differ from a plain program's by a relative error of at most 0.0006.
Values may be sent and summed in bfloat16 or wider, within the bound.
No kernel may reach another device: no remote copies, remote signals or barrier semaphores. Data moves between devices by JAX's collectives and lax.ppermute only.
A program may use at most 128 MiB of HBM per device.

v0:
```python
import math
import jax
import jax.numpy as jnp
from jax import lax
from jax.sharding import PartitionSpec as P

PRECISE = lax.Precision.HIGHEST


def shifted(value, axis, by):
    peers = lax.axis_size(axis)
    pairs = [(i, i + by) for i in range(peers) if 0 <= i + by < peers]
    return lax.ppermute(value, axis, pairs)


def position_features(position, sequence, feature_rows):
    bands = jnp.arange(feature_rows // 2, dtype=jnp.int32)
    factor = 4 * (bands + 1) * (bands + 1)
    phase = position[None, :] * factor[:, None] % sequence
    angles = 2.0 * math.pi / sequence * phase.astype(jnp.float32)
    return jnp.concatenate([jnp.cos(angles), jnp.sin(angles)], axis=0)


def angle_tables(left_index, right_index, modulus):
    phase = left_index[:, None] * right_index[None, :] % modulus
    angles = 2.0 * math.pi / modulus * phase.astype(jnp.float32)
    return (jnp.cos(angles), jnp.sin(angles))


def contract(form, left, right):
    return jnp.einsum(form, left, right, precision=PRECISE)


def times_forward(real_part, imag_part, cosine, sine):
    return (real_part * cosine + imag_part * sine, imag_part * cosine - real_part * sine)


def times_inverse(real_part, imag_part, cosine, sine):
    return (real_part * cosine - imag_part * sine, imag_part * cosine + real_part * sine)


def complex_times(first_real, first_imag, second_real, second_imag):
    return (
        first_real * second_real - first_imag * second_imag,
        first_real * second_imag + first_imag * second_real,
    )


def local_forward(real_part, imag_part):
    length = real_part.shape[-1]
    inner = 64
    outer = length // inner
    leading = real_part.shape[:-1]
    real_part = real_part.reshape(leading + (outer, inner))
    imag_part = imag_part.reshape(leading + (outer, inner))
    outer_index = jnp.arange(outer, dtype=jnp.int32)
    inner_index = jnp.arange(inner, dtype=jnp.int32)
    cos_outer, sin_outer = angle_tables(outer_index, outer_index, outer)
    first_real = contract("cb,...ba->...ca", cos_outer, real_part) + contract(
        "cb,...ba->...ca", sin_outer, imag_part
    )
    first_imag = contract("cb,...ba->...ca", cos_outer, imag_part) - contract(
        "cb,...ba->...ca", sin_outer, real_part
    )
    cos_middle, sin_middle = angle_tables(outer_index, inner_index, length)
    first_real, first_imag = times_forward(first_real, first_imag, cos_middle, sin_middle)
    cos_inner, sin_inner = angle_tables(inner_index, inner_index, inner)
    final_real = contract("...ca,da->...cd", first_real, cos_inner) + contract(
        "...ca,da->...cd", first_imag, sin_inner
    )
    final_imag = contract("...ca,da->...cd", first_imag, cos_inner) - contract(
        "...ca,da->...cd", first_real, sin_inner
    )
    return (final_real, final_imag)


def local_inverse(real_part, imag_part):
    outer = real_part.shape[-2]
    inner = real_part.shape[-1]
    length = outer * inner
    leading = real_part.shape[:-2]
    outer_index = jnp.arange(outer, dtype=jnp.int32)
    inner_index = jnp.arange(inner, dtype=jnp.int32)
    cos_inner, sin_inner = angle_tables(inner_index, inner_index, inner)
    first_real = contract("...cd,ad->...ca", real_part, cos_inner) - contract(
        "...cd,ad->...ca", imag_part, sin_inner
    )
    first_imag = contract("...cd,ad->...ca", imag_part, cos_inner) + contract(
        "...cd,ad->...ca", real_part, sin_inner
    )
    cos_middle, sin_middle = angle_tables(outer_index, inner_index, length)
    first_real, first_imag = times_inverse(first_real, first_imag, cos_middle, sin_middle)
    cos_outer, sin_outer = angle_tables(outer_index, outer_index, outer)
    final_real = contract("bc,...ca->...ba", cos_outer, first_real) - contract(
        "bc,...ca->...ba", sin_outer, first_imag
    )
    final_imag = contract("bc,...ca->...ba", cos_outer, first_imag) + contract(
        "bc,...ca->...ba", sin_outer, first_real
    )
    return (final_real.reshape(leading + (length,)), final_imag.reshape(leading + (length,)))


def held_frequencies(device):
    return 2 * device + jnp.arange(2, dtype=jnp.int32)


def forward_spectrum(signals):
    shards = lax.axis_size("ctx")
    device = lax.axis_index("ctx")
    signal_count, channels, length = signals.shape
    padded = 2 * shards * length
    columns = lax.all_to_all(
        signals.reshape((1, signal_count, channels, length)),
        "ctx",
        split_axis=3,
        concat_axis=0,
        tiled=True,
    )
    shard_index = jnp.arange(shards, dtype=jnp.int32)
    freq_index = jnp.arange(2 * shards, dtype=jnp.int32)
    cos_table, sin_table = angle_tables(freq_index, shard_index, 2 * shards)
    rows_real = contract("qp,pmgb->qmgb", cos_table, columns)
    rows_imag = -contract("qp,pmgb->qmgb", sin_table, columns)
    arrived = lax.all_to_all(
        jnp.stack([rows_real, rows_imag]), "ctx", split_axis=1, concat_axis=4, tiled=True
    )
    spec_real = arrived[0]
    spec_imag = arrived[1]
    freqs = held_frequencies(device)
    cosine, sine = angle_tables(freqs, jnp.arange(length, dtype=jnp.int32), padded)
    spec_real, spec_imag = times_forward(
        spec_real, spec_imag, cosine[:, None, None, :], sine[:, None, None, :]
    )
    return local_forward(spec_real, spec_imag)


def inverse_columns(spec_real, spec_imag):
    shards = lax.axis_size("ctx")
    device = lax.axis_index("ctx")
    real_part, imag_part = local_inverse(spec_real, spec_imag)
    length = real_part.shape[-1]
    padded = 2 * shards * length
    freqs = held_frequencies(device)
    cosine, sine = angle_tables(freqs, jnp.arange(length, dtype=jnp.int32), padded)
    real_part, imag_part = times_inverse(
        real_part, imag_part, cosine[:, None, None, :], sine[:, None, None, :]
    )
    shard_index = jnp.arange(shards, dtype=jnp.int32)
    arrived = lax.all_to_all(
        jnp.stack([real_part, imag_part]), "ctx", split_axis=4, concat_axis=1, tiled=True
    )
    cos_table, sin_table = angle_tables(
        shard_index, jnp.arange(2 * shards, dtype=jnp.int32), 2 * shards
    )
    columns = contract("pq,qmgb->pmgb", cos_table, arrived[0]) - contract(
        "pq,qmgb->pmgb", sin_table, arrived[1]
    )
    return columns * (1.0 / padded)


def to_tokens(columns):
    arrived = lax.all_to_all(columns, "ctx", split_axis=0, concat_axis=3, tiled=True)
    return arrived[0]


def body(
    query_in,
    key_in,
    value_in,
    short_kernel,
    filter_in,
    filter_out,
    filter_decay,
    skip_gain,
    grad_out,
):
    shards = lax.axis_size("ctx")
    device = lax.axis_index("ctx")
    length = query_in.shape[1]
    sequence = shards * length
    scale = sequence ** (-0.5)
    inputs = jnp.stack([query_in, key_in, value_in])
    rim = shifted(inputs[:, :, -2:], "ctx", 1)
    values = inputs.astype(jnp.float32)
    rim_values = rim.astype(jnp.float32)
    before_one = jnp.concatenate([rim_values[..., 1:], values[..., :-1]], axis=-1)
    before_two = jnp.concatenate([rim_values, values[..., :-2]], axis=-1)
    kernel = short_kernel[:, :, :, None]
    shorted = kernel[:, 0] * values + kernel[:, 1] * before_one + kernel[:, 2] * before_two
    query_short = shorted[0]
    key_short = shorted[1]
    value_short = shorted[2]
    gate = key_short * value_short
    position = device * length + jnp.arange(length, dtype=jnp.int32)
    fraction = position.astype(jnp.float32) / sequence
    basis = position_features(position, sequence, filter_in.shape[0])
    preact = jnp.dot(filter_in.T, basis, precision=PRECISE)
    hidden = jnp.sin(preact)
    window = jnp.exp(-filter_decay[:, None] * fraction[None, :])
    taps = window * jnp.dot(filter_out.T, hidden, precision=PRECISE) * scale
    spec_real, spec_imag = forward_spectrum(jnp.stack([gate, taps]))
    gate_real, gate_imag = (spec_real[:, 0], spec_imag[:, 0])
    taps_real, taps_imag = (spec_real[:, 1], spec_imag[:, 1])
    prod_real, prod_imag = complex_times(gate_real, gate_imag, taps_real, taps_imag)
    conv = to_tokens(inverse_columns(prod_real[:, None], prod_imag[:, None]))[0]
    mixed = conv + skip_gain[:, None] * gate
    output = (query_short * mixed).astype(jnp.bfloat16)
    upstream = grad_out.astype(jnp.float32)
    grad_mixed = upstream * query_short
    grad_query_short = upstream * mixed
    upper_real, upper_imag = forward_spectrum(grad_mixed[None])
    upper_real = upper_real[:, 0]
    upper_imag = upper_imag[:, 0]
    along_real, along_imag = complex_times(taps_real, -taps_imag, upper_real, upper_imag)
    cross_real, cross_imag = complex_times(gate_real, -gate_imag, upper_real, upper_imag)
    backward = to_tokens(
        inverse_columns(
            jnp.stack([along_real, cross_real], axis=1), jnp.stack([along_imag, cross_imag], axis=1)
        )
    )
    grad_gate = backward[0] + skip_gain[:, None] * grad_mixed
    grad_taps = backward[1]
    grads = jnp.stack([grad_query_short, grad_gate * value_short, grad_gate * key_short])
    after = shifted(grads[..., :2], "ctx", -1)
    next_one = jnp.concatenate([grads[..., 1:], after[..., :1]], axis=-1)
    next_two = jnp.concatenate([grads[..., 2:], after], axis=-1)
    grad_inputs = (kernel[:, 0] * grads + kernel[:, 1] * next_one + kernel[:, 2] * next_two).astype(
        jnp.bfloat16
    )
    short_terms = jnp.stack(
        [
            jnp.sum(grads * values, axis=-1),
            jnp.sum(grads * before_one, axis=-1),
            jnp.sum(grads * before_two, axis=-1),
        ],
        axis=1,
    )
    weighted = grad_taps * window * scale
    out_terms = jnp.dot(hidden, weighted.T, precision=PRECISE)
    grad_hidden = jnp.dot(filter_out, weighted, precision=PRECISE)
    in_terms = jnp.dot(basis, (grad_hidden * jnp.cos(preact)).T, precision=PRECISE)
    decay_terms = jnp.sum(grad_taps * taps * -fraction[None, :], axis=1)
    skip_terms = jnp.sum(grad_mixed * gate, axis=1)
    short_sum, out_sum, decay_sum, skip_sum = lax.psum(
        (short_terms, out_terms, decay_terms, skip_terms), "ctx"
    )
    in_sum = lax.psum(in_terms, ("ctx", "chan"))
    return (
        output,
        grad_inputs[0],
        grad_inputs[1],
        grad_inputs[2],
        short_sum * scale,
        in_sum * scale,
        out_sum * scale,
        decay_sum * scale,
        skip_sum * scale,
    )


def solution(mesh):
    placed = (
        P("chan", "ctx"),
        P("chan", "ctx"),
        P("chan", "ctx"),
        P(None, None, "chan"),
        P(),
        P(None, "chan"),
        P("chan"),
        P("chan"),
        P("chan", "ctx"),
    )
    return jax.shard_map(
        body,
        mesh=mesh,
        in_specs=placed,
        out_specs=(
            P("chan", "ctx"),
            P("chan", "ctx"),
            P("chan", "ctx"),
            P("chan", "ctx"),
            P(None, None, "chan"),
            P(),
            P(None, "chan"),
            P("chan"),
            P("chan"),
        ),
        check_vma=False,
    )
```

profile of v0, /device:TPU:0, one launch (start us, length us, event | category | flops | bytes accessed | tf_op | source)
XLA Modules:
  0.0 651.2 jit_solution(13803028707653949594)
XLA Ops:
  11.0 4.8 collective-permute-start
  20.5 6.6 %all-to-all-start.4 = ((f32[1,1,1024,128]{2,1,0,3:T(1,128)}), f32[1,1,1024,128]{2,1,0,3:T(1,128)}, u32[]{:S(2)}, u32[]{:S(2)}) async-start(f32[1,1,1024,128]{2,1,0,3:T(1,128)} %copy.246), calls=%async_computation.4 | async-start | bytes 1048576 | tf_op jit(solution)/shard_map/all_to_all | solution.py:112
  32.8 7.8 %all-to-all-done.4 = f32[1,1,1024,128]{2,1,0,3:T(1,128)} async-done(((f32[1,1,1024,128]{2,1,0,3:T(1,128)}), f32[1,1,1024,128]{2,1,0,3:T(1,128)}, u32[]{:S(2)}, u32[]{:S(2)}) %all-to-all-start.4) | async-done | bytes 524320 | tf_op jit(solution)/shard_map/all_to_all | solution.py:112
  40.6 4.2 all-to-all-start
  51.2 18.4 %all-to-all-done = f32[1,2,1024,128]{2,1,0,3:T(2,128)} async-done(((f32[1,2,1024,128]{2,1,0,3:T(2,128)}), f32[1,2,1024,128]{2,1,0,3:T(2,128)}, u32[]{:S(2)}, u32[]{:S(2)}) %all-to-all-start) | async-done | bytes 1048608 | tf_op jit(solution)/shard_map/all_to_all | solution.py:112
  69.6 4.8 all-to-all-start.5
  74.4 3.4 negate_bitcast_fusion
  77.9 3.4 convolution_bitcast_fusion
  81.9 4.4 copy.220
  86.3 35.7 %all-to-all-done.5 = f32[2,16,1,1024,16]{3,4,2,0,1:T(8,128)} async-done(((f32[2,16,1,1024,16]{3,4,2,0,1:T(8,128)}), f32[2,16,1,1024,16]{3,4,2,0,1:T(8,128)}, u32[]{:S(2)}, u32[]{:S(2)}) %all-to-all-start.5) | async-done | bytes 2097184 | tf_op jit(solution)/shard_map/all_to_all | solution.py:124
  122.0 4.7 all-to-all-start.1
  132.9 4.1 fusion.61
  136.9 4.3 fusion.35
  141.3 4.1 fusion.65
  145.3 5.7 subtract_bitcast_fusion.1
  157.5 61.7 %all-to-all-done.1 = f32[2,16,2,1024,16]{3,4,2,0,1:T(8,128)} async-done(((f32[2,16,2,1024,16]{3,4,2,0,1:T(8,128)}), f32[2,16,2,1024,16]{3,4,2,0,1:T(8,128)}, u32[]{:S(2)}, u32[]{:S(2)}) %all-to-all-start.1) | async-done | bytes 4194336 | tf_op jit(solution)/shard_map/all_to_all | solution.py:124
  224.1 7.9 %fusion.26 = f32[2,2,1024,64,2]{2,4,3,1,0:T(2,128)S(1)} fusion(f32[2,2,1024,2,64]{2,4,3,1,0:T(8,128)S(1)} %get-tuple-element.68), kind=kOutput, calls=%fused_computation.48 | convolution fusion | flops 12582968 | bytes 4194304 | tf_op jit(solution)/shard_map/cb,...ba->...ca/dot_general | solution.py:31
  232.0 8.3 %fusion.22 = f32[2,2,1024,64,2]{2,4,3,1,0:T(2,128)S(1)} fusion(f32[2,2,1024,2,64]{2,4,3,1,0:T(8,128)S(1)} %get-tuple-element.69), kind=kOutput, calls=%fused_computation.44 | convolution fusion | flops 12582968 | bytes 4194304 | tf_op jit(solution)/shard_map/cb,...ba->...ca/dot_general | solution.py:31
  240.3 8.2 %convolution_add_fusion = f32[2,2,1024,64,2]{2,4,3,1,0:T(2,128)S(1)} fusion(f32[2,2,1024,64,2]{2,4,3,1,0:T(2,128)S(1)} %fusion.26, f32[2,2,1024,2,64]{2,4,3,1,0:T(8,128)S(1)} %get-tuple-element.69), kind=kOutput, calls=%fused_computation.42 | convolution fusion | flops 13107256 | bytes 6291456 | tf_op jit(solution)/shard_map/cb,...ba->...ca/dot_general | solution.py:31
  248.6 11.2 %fusion.2 = (f32[2,2,1024,2,64]{2,3,4,1,0:T(2,128)S(1)}, f32[2,2,1024,2,64]{2,3,4,1,0:T(2,128)S(1)}) fusion(f32[2,2,1024,64,2]{2,4,3,1,0:T(2,128)S(1)} %convolution_add_fusion, f32[2,64]{0,1:T(8,128)S(1)} %copy-done.21, f32[2,64]{0,1:T(8,128)S(1)} %copy-done.23, f32[2,2,1024,64,2]{2,4,3,1,0:T(2,128)S(1)} %fusion.22, ...), kind=kOutput, calls=%fused_computation.14 | convolution fusion | flops 16252984 | bytes 10486784 | tf_op jit(solution)/shard_map/cb,...ba->...ca/dot_general | solution.py:31
  265.4 3.1 fusion.16
  268.6 3.1 fusion.19
  271.7 3.9 multiply_subtract_fusion.3
  284.9 9.6 %multiply_subtract_fusion = (f32[2,2,1024,2,64]{2,3,4,1,0:T(2,128)S(1)}, f32[2,2,1024,2,64]{2,3,4,1,0:T(2,128)S(1)}) fusion(f32[2,64]{0,1:T(8,128)S(1)} %copy-done.21, f32[2,64]{0,1:T(8,128)S(1)} %copy-done.23, f32[2,2,1024,2,64]{2,4,3,1,0:T(8,128)S(1)} %fusion.13, f32[2,2,1024,2,64]{2,4,3,1,0:T(8,128)S(1)} %fusion.15, ...), kind=kLoop, calls=%fused_computation.23 | loop fusion | flops 4194304 | bytes 12583936 | tf_op jit(solution)/shard_map/sub | solution.py:39
  294.5 7.5 %fusion.190 = f32[2,2,1024,64,2]{2,4,3,1,0:T(2,128)S(1)} fusion(f32[2,2,1024,2,64]{2,3,4,1,0:T(2,128)S(1)} %get-tuple-element.60), kind=kOutput, calls=%fused_computation.283 | convolution fusion | flops 12582968 | bytes 4194304 | tf_op jit(solution)/shard_map/bc,...ca->...ba/dot_general | solution.py:31
  302.0 7.5 %fusion.188 = f32[2,2,1024,64,2]{2,4,3,1,0:T(2,128)S(1)} fusion(f32[2,2,1024,2,64]{2,3,4,1,0:T(2,128)S(1)} %get-tuple-element.61), kind=kOutput, calls=%fused_computation.281 | convolution fusion | flops 12582968 | bytes 4194304 | tf_op jit(solution)/shard_map/bc,...ca->...ba/dot_general | solution.py:31
  309.6 8.4 %subtract_bitcast_fusion = f32[2,2,1024,2,64]{2,3,4,1,0:T(2,128)S(1)} fusion(f32[2,2,1024,64,2]{2,4,3,1,0:T(2,128)S(1)} %fusion.190, f32[2,2,1024,2,64]{2,3,4,1,0:T(2,128)S(1)} %get-tuple-element.61), kind=kOutput, calls=%fused_computation.21 | convolution fusion | flops 13107256 | bytes 6291456 | tf_op jit(solution)/shard_map/bc,...ca->...ba/dot_general | solution.py:31
  317.9 8.0 %add_bitcast_fusion = f32[2,2,1024,2,64]{2,3,4,1,0:T(2,128)S(1)} fusion(f32[2,2,1024,64,2]{2,4,3,1,0:T(2,128)S(1)} %fusion.188, f32[2,2,1024,2,64]{2,3,4,1,0:T(2,128)S(1)} %get-tuple-element.60), kind=kOutput, calls=%fused_computation.20 | convolution fusion | flops 13107256 | bytes 6291456 | tf_op jit(solution)/shard_map/bc,...ca->...ba/dot_general | solution.py:31
  328.8 5.2 copy.268
  334.0 5.0 all-to-all-start.6
  345.8 4.1 fusion.67
  349.8 4.3 fusion.37
  354.5 4.1 fusion.71
  358.5 4.4 fusion.38
  366.8 64.8 %all-to-all-done.6 = f32[2,2,2,1024,128]{3,2,1,0,4:T(2,128)} async-done(((f32[2,2,2,1024,128]{3,2,1,0,4:T(2,128)}), f32[2,2,2,1024,128]{3,2,1,0,4:T(2,128)}, u32[]{:S(2)}, u32[]{:S(2)}) %all-to-all-start.6) | async-done | bytes 4194336 | tf_op jit(solution)/shard_map/all_to_all | solution.py:149
  431.5 4.4 all-to-all-start.2
  435.9 4.6 copy.269
  445.3 3.7 squeeze.65
  449.1 4.6 copy.270
  453.7 3.7 squeeze.64
  462.9 20.8 %all-to-all-done.2 = f32[2,2,1,1024,128]{3,1,2,0,4:T(2,128)} async-done(((f32[2,2,1,1024,128]{3,1,2,0,4:T(2,128)}), f32[2,2,1,1024,128]{3,1,2,0,4:T(2,128)}, u32[]{:S(2)}, u32[]{:S(2)}) %all-to-all-start.2) | async-done | bytes 2097184 | tf_op jit(solution)/shard_map/all_to_all | solution.py:149
  483.7 4.5 all-to-all-start.7
  496.9 3.0 copy.242
  506.5 7.3 %all-to-all-done.7 = f32[8,2,1024,16]{2,3,1,0:T(8,128)} async-done(((f32[8,2,1024,16]{2,3,1,0:T(8,128)}), f32[8,2,1024,16]{2,3,1,0:T(8,128)}, u32[]{:S(2)}, u32[]{:S(2)}) %all-to-all-start.7) | async-done | bytes 1048608 | tf_op jit(solution)/shard_map/all_to_all | solution.py:162
  513.8 4.1 all-to-all-start.3
  523.4 40.9 %psum.36 = f32[64,64]{1,0:T(8,128)S(1)} all-reduce(f32[64,64]{1,0:T(8,128)} %fusion.105), channel_id=1, replica_groups=mesh['ctx'=8,'chan'=4] {'ctx','chan'}, use_global_device_ids=true, to_apply=%region_4.5 | all-reduce | flops 4096 | bytes 32768 | tf_op jit(solution)/shard_map/psum | solution.py:247
  574.1 37.3 %all-reduce = (f32[3,3,1024]{2,0,1:T(4,128)S(1)}, f32[1024]{0:T(1024)S(1)}, f32[1024]{0:T(1024)S(1)}) all-reduce(f32[3,3,1024]{2,0,1:T(4,128)S(1)} %pad_maximum_fusion.14, f32[1024]{0:T(1024)S(1)} %get-tuple-element.106, f32[1024]{0:T(1024)S(1)} %get-tuple-element.96), channel_id=1, replica_groups=mesh['ctx'=8,'chan'=4] {'ctx'}, use_global_device_ids=true, to_apply=%region_3.4 | all-reduce | flops 11264 | bytes 90112 | tf_op jit(solution)/shard_map/psum | solution.py:244
  621.0 21.3 %all-reduce.3.cloned.1.call-done = f32[64,1024]{1,0:T(8,128)} async-done(((f32[64,1024]{1,0:T(8,128)}), f32[64,1024]{1,0:T(8,128)}) %all-reduce.3.cloned.1.call-update) | async-done | bytes 262160 | tf_op jit(solution)/shard_map/psum | solution.py:244
  (188 shorter events, 118.8 us)
Async XLA Ops:
  7.2 22.2 %copy-start = (f32[64,1024]{1,0:T(8,128)S(1)}, f32[64,1024]{1,0:T(8,128)}, u32[]{:S(2)}) copy-start(f32[64,1024]{1,0:T(8,128)} %param.14) | copy-start | bytes 786436
  8.3 2.6 copy-start.10
  8.3 7.5 %copy-start.27 = (f32[3,3,1024]{2,1,0:T(4,128)S(1)}, f32[3,3,1024]{2,1,0:T(4,128)}, u32[]{:S(2)}) copy-start(f32[3,3,1024]{2,1,0:T(4,128)} %param.12) | copy-start | bytes 110596
  8.3 7.7 %copy-start.36 = (f32[1024]{0:T(1024)S(1)}, f32[1024]{0:T(1024)}, u32[]{:S(2)}) copy-start(f32[1024]{0:T(1024)} %param.15) | copy-start | bytes 12292
  8.4 7.8 %copy-start.19 = (bf16[1024,128]{1,0:T(8,128)(2,1)S(1)}, bf16[1024,128]{1,0:T(8,128)(2,1)}, u32[]{:S(2)}) copy-start(bf16[1024,128]{1,0:T(8,128)(2,1)} %param.17) | copy-start | bytes 786436
  9.6 7.4 %copy-start.11 = (bf16[1024,128]{0,1:T(8,128)(2,1)}, bf16[1024,128]{0,1:T(8,128)(2,1)S(1)}, u32[]{:S(2)}) copy-start(bf16[1024,128]{0,1:T(8,128)(2,1)S(1)} %copy.215) | copy-start | bytes 786436
  10.8 6.5 copy-start.12
  11.0 6.2 collective-permute-start
  17.3 1.8 copy-start.25
  17.3 1.7 copy-start.18
  20.5 20.0 %all-to-all-start.4 = ((f32[1,1,1024,128]{2,1,0,3:T(1,128)}), f32[1,1,1024,128]{2,1,0,3:T(1,128)}, u32[]{:S(2)}, u32[]{:S(2)}) async-start(f32[1,1,1024,128]{2,1,0,3:T(1,128)} %copy.246), calls=%async_computation.4 | async-start | bytes 1048576 | tf_op jit(solution)/shard_map/all_to_all | solution.py:112
  27.7 1.7 copy-start.37
  30.1 0.8 copy-start.8
  40.6 29.0 %all-to-all-start = ((f32[1,2,1024,128]{2,1,0,3:T(2,128)}), f32[1,2,1024,128]{2,1,0,3:T(2,128)}, u32[]{:S(2)}, u32[]{:S(2)}) async-start(f32[1,2,1024,128]{2,1,0,3:T(2,128)} %copy.217), calls=%async_computation | async-start | bytes 2097152 | tf_op jit(solution)/shard_map/all_to_all | solution.py:112
  69.6 52.4 %all-to-all-start.5 = ((f32[2,16,1,1024,16]{3,4,2,0,1:T(8,128)}), f32[2,16,1,1024,16]{3,4,2,0,1:T(8,128)}, u32[]{:S(2)}, u32[]{:S(2)}) async-start(f32[2,16,1,1024,16]{3,4,2,0,1:T(8,128)} %copy.248), calls=%async_computation.5 | async-start | bytes 4194304 | tf_op jit(solution)/shard_map/all_to_all | solution.py:124
  122.0 97.3 %all-to-all-start.1 = ((f32[2,16,2,1024,16]{3,4,2,0,1:T(8,128)}), f32[2,16,2,1024,16]{3,4,2,0,1:T(8,128)}, u32[]{:S(2)}, u32[]{:S(2)}) async-start(f32[2,16,2,1024,16]{3,4,2,0,1:T(8,128)} %copy.220), calls=%async_computation.1 | async-start | bytes 8388608 | tf_op jit(solution)/shard_map/all_to_all | solution.py:124
  127.4 2.1 copy-start.30
  130.3 2.2 copy-start.28
  141.2 4.1 copy-start.20
  141.2 4.1 copy-start.22
  151.1 4.0 copy-start.15
  222.6 0.7 copy-start.29
  240.3 8.3 %copy-start.21 = (f32[2,64]{0,1:T(8,128)S(1)}, f32[2,64]{0,1:T(8,128)}, u32[]{:S(2)}) copy-start(f32[2,64]{0,1:T(8,128)} %copy.229) | copy-start | bytes 1540
  240.3 8.3 %copy-start.23 = (f32[2,64]{0,1:T(8,128)S(1)}, f32[2,64]{0,1:T(8,128)}, u32[]{:S(2)}) copy-start(f32[2,64]{0,1:T(8,128)} %copy.226) | copy-start | bytes 1540
  268.5 3.1 copy-start.14
  268.6 3.1 copy-start.16
  268.6 3.1 copy-start.17
  326.5 0.7 copy-start.33
  334.0 97.5 %all-to-all-start.6 = ((f32[2,2,2,1024,128]{3,2,1,0,4:T(2,128)}), f32[2,2,2,1024,128]{3,2,1,0,4:T(2,128)}, u32[]{:S(2)}, u32[]{:S(2)}) async-start(f32[2,2,2,1024,128]{3,2,1,0,4:T(2,128)} %copy.268), calls=%async_computation.6 | async-start | bytes 8388608 | tf_op jit(solution)/shard_map/all_to_all | solution.py:149
  339.0 2.6 copy-start.1
  339.0 3.8 copy-start.2
  342.9 1.3 copy-start.31
  342.9 1.3 copy-start.32
  358.5 4.7 copy-start.35
  431.5 52.2 %all-to-all-start.2 = ((f32[2,2,1,1024,128]{3,1,2,0,4:T(2,128)}), f32[2,2,1,1024,128]{3,1,2,0,4:T(2,128)}, u32[]{:S(2)}, u32[]{:S(2)}) async-start(f32[2,2,1,1024,128]{3,1,2,0,4:T(2,128)} %copy.240), calls=%async_computation.2 | async-start | bytes 4194304 | tf_op jit(solution)/shard_map/all_to_all | solution.py:149
  457.3 2.9 copy-start.3
  483.7 30.1 %all-to-all-start.7 = ((f32[8,2,1024,16]{2,3,1,0:T(8,128)}), f32[8,2,1024,16]{2,3,1,0:T(8,128)}, u32[]{:S(2)}, u32[]{:S(2)}) async-start(f32[8,2,1024,16]{2,3,1,0:T(8,128)} %copy.272), calls=%async_computation.7 | async-start | bytes 2097152 | tf_op jit(solution)/shard_map/all_to_all | solution.py:162
  502.8 2.0 copy-start.13
  513.8 53.3 %all-to-all-start.3 = ((f32[8,1,1024,16]{2,3,1,0:T(8,128)}), f32[8,1,1024,16]{2,3,1,0:T(8,128)}, u32[]{:S(2)}, u32[]{:S(2)}) async-start(f32[8,1,1024,16]{2,3,1,0:T(8,128)} %copy.244), calls=%async_computation.3 | async-start | bytes 1048576 | tf_op jit(solution)/shard_map/all_to_all | solution.py:162
  517.9 124.3 %all-reduce.3.cloned.1.call-start = ((), (), s32[]{:S(2)}) async-start(), calls=%async_computation.8 | async-start | bytes 524288 | tf_op jit(solution)/shard_map/psum | solution.py:244
  518.0 2.2 copy-start.9
  518.0 3.9 copy-start.24
  521.1 0.8 copy-start.7
  567.0 4.7 copy-start.26
  612.0 5.7 collective-permute-start.1
  614.1 3.7 copy-start.4
  614.1 3.7 copy-start.5
  614.1 3.7 copy-start.6
  (1 other events, 0.7 us)
Sparse Core Ops, SparseCore 0:
  571.8 70.4 all-reduce.2
where the time goes:
time: 659 us; the launch traced here: 651 us
  waiting for transfers between devices  241 us (37%)
  matrix products  162 us (25%)
  local copies, waits for them, and re-layouts  82.3 us (12%)
  blocking collectives  78.2 us (12%)
  starting transfers between devices  44.5 us (7%)
  other arithmetic  28.1 us (4%)
  between operations  15.7 us (2%)
    dot_general x40, matrix products, contract(): return jnp.einsum(form, left, right, precision=PRECISE)  156 us
    all_to_all x2, waiting for transfers between devices, forward_spectrum(): lax.all_to_all(jnp.stack([rows_real, rows_imag]), 'ctx', split_axis=1, co...  97.4 us
    all_to_all x2, waiting for transfers between devices, inverse_columns(): lax.all_to_all(jnp.stack([real_part, imag_part]), 'ctx', split_axis=4, co...  85.6 us
    psum x1, blocking collectives, body(): in_sum = lax.psum(in_terms, ('ctx', 'chan'))  40.9 us
    psum x1, blocking collectives, body(): lax.psum((short_terms, out_terms, decay_terms, skip_terms), 'ctx')  37.3 us
    all_to_all x2, waiting for transfers between devices, forward_spectrum(): lax.all_to_all(signals.reshape((1, signal_count, channels, length)), 'ctx...  26.2 us
    psum x1, waiting for transfers between devices, body(): lax.psum((short_terms, out_terms, decay_terms, skip_terms), 'ctx')  21.3 us
  transfers between devices with their start and end apart: 11, of which 10 were waited for; matrix products, arithmetic and copies ran while one was open for 22% of the time, Pallas kernels for 0%

commit v1 on v0

--- a/solution.py
+++ b/solution.py
@@ -5,6 +5,29 @@
 from jax.sharding import PartitionSpec as P
 
 PRECISE = lax.Precision.HIGHEST
+
+
+def cut_along(array, dim, size):
+    dims = array.shape
+    tiles = array.reshape(*dims[:dim], size, dims[dim] // size, *dims[dim + 1 :])
+    return jnp.moveaxis(tiles, dim, 0)
+
+
+def laid_out(pieces, dim):
+    shape = list(pieces.shape[1:])
+    shape[dim] *= pieces.shape[0]
+    return jnp.moveaxis(pieces, 0, dim).reshape(shape)
+
+
+def swapped_with_each(shard, axis, split_dim, concat_dim):
+    count, index = (lax.axis_size(axis), lax.axis_index(axis))
+    blocks = cut_along(shard, split_dim, count)
+    outs = [blocks[index]]
+    for turn in range(1, count):
+        sent = blocks[index ^ turn]
+        outs.append(lax.ppermute(sent, axis, [(i, i ^ turn) for i in range(count)]))
+    blocks = jnp.stack(outs)[index ^ jnp.arange(count)]
+    return laid_out(blocks, concat_dim)
 
 
 def shifted(value, axis, by):
@@ -121,9 +144,7 @@
     cos_table, sin_table = angle_tables(freq_index, shard_index, 2 * shards)
     rows_real = contract("qp,pmgb->qmgb", cos_table, columns)
     rows_imag = -contract("qp,pmgb->qmgb", sin_table, columns)
-    arrived = lax.all_to_all(
-        jnp.stack([rows_real, rows_imag]), "ctx", split_axis=1, concat_axis=4, tiled=True
-    )
+    arrived = swapped_with_each(jnp.stack([rows_real, rows_imag]), "ctx", 1, 4)
     spec_real = arrived[0]
     spec_imag = arrived[1]
     freqs = held_frequencies(device)

time: 659 us -> 743 us (1.13)
  starting transfers between devices: 44.5 us -> 93.4 us
  waiting for transfers between devices: 241 us -> 282 us
  matrix products: 162 us -> 153 us
    all_to_all x2 -> x0, waiting for transfers between devices: 97.4 us -> none  [forward_spectrum(): lax.all_to_all(jnp.stack([rows_real, rows_imag]), 'ctx', split_axis=1, co...]
    ppermute x0 -> x14, waiting for transfers between devices: none -> 91.5 us  [swapped_with_each(): outs.append(lax.ppermute(sent, axis, [(i, i ^ turn) for i in range(count)]))]
    psum x1, waiting for transfers between devices: 21.3 us -> 66.1 us  [body(): lax.psum((short_terms, out_terms, decay_terms, skip_terms), 'ctx')]
    ppermute x0 -> x14, starting transfers between devices: none -> 43.8 us  [swapped_with_each(): outs.append(lax.ppermute(sent, axis, [(i, i ^ turn) for i in range(count)]))]
    all_to_all x2, waiting for transfers between devices: 7.28 us -> 28 us  [to_tokens(): lax.all_to_all(columns, 'ctx', split_axis=0, concat_axis=3, tiled=True)]
    all_to_all x2, starting transfers between devices: 9.33 us -> 25.8 us  [inverse_columns(): lax.all_to_all(jnp.stack([real_part, imag_part]), 'ctx', split_axis=4, co...]
    all_to_all x2, waiting for transfers between devices: 26.2 us -> 9.97 us  [forward_spectrum(): lax.all_to_all(signals.reshape((1, signal_count, channels, length)), 'ctx...]
    all_to_all x2 -> x0, starting transfers between devices: 9.55 us -> none  [forward_spectrum(): lax.all_to_all(jnp.stack([rows_real, rows_imag]), 'ctx', split_axis=1, co...]
  transfers between devices with their start and end apart: 11 -> 23, of which waited for: 10 -> 13; matrix products, arithmetic and copies ran while one was open for 22% -> 17% of each run, Pallas kernels for 0% -> 0%
where the time goes in v1:
time: 743 us; the launch traced here: 738 us
  waiting for transfers between devices  282 us (38%)
  matrix products  153 us (21%)
  starting transfers between devices  93.4 us (13%)
  local copies, waits for them, and re-layouts  83.7 us (11%)
  blocking collectives  74.8 us (10%)
  other arithmetic  34.8 us (5%)
  between operations  15.9 us (2%)
    dot_general x40, matrix products, contract(): return jnp.einsum(form, left, right, precision=PRECISE)  149 us
    ppermute x14, waiting for transfers between devices, swapped_with_each(): outs.append(lax.ppermute(sent, axis, [(i, i ^ turn) for i in range(count)]))  91.5 us
    all_to_all x2, waiting for transfers between devices, inverse_columns(): lax.all_to_all(jnp.stack([real_part, imag_part]), 'ctx', split_axis=4, co...  86.8 us
    psum x1, waiting for transfers between devices, body(): lax.psum((short_terms, out_terms, decay_terms, skip_terms), 'ctx')  66.1 us
    ppermute x14, starting transfers between devices, swapped_with_each(): outs.append(lax.ppermute(sent, axis, [(i, i ^ turn) for i in range(count)]))  43.8 us
    psum x1, blocking collectives, body(): in_sum = lax.psum(in_terms, ('ctx', 'chan'))  39.2 us
    psum x1, blocking collectives, body(): lax.psum((short_terms, out_terms, decay_terms, skip_terms), 'ctx')  35.7 us
    all_to_all x2, waiting for transfers between devices, to_tokens(): lax.all_to_all(columns, 'ctx', split_axis=0, concat_axis=3, tiled=True)  28 us
  transfers between devices with their start and end apart: 23, of which 13 were waited for; matrix products, arithmetic and copies ran while one was open for 17% of the time, Pallas kernels for 0%

profile of v1, /device:TPU:0, one launch (start us, length us, event | category | flops | bytes accessed | tf_op | source)
XLA Modules:
  0.0 737.8 jit_solution(18120003627878602156)
XLA Ops:
  11.0 4.8 collective-permute-start
  23.9 4.9 all-to-all-start.3
  33.1 10.0 %all-to-all-done.3 = f32[1,1,1024,128]{2,1,0,3:T(1,128)S(1)} async-done(((f32[1,1,1024,128]{2,1,0,3:T(1,128)}), f32[1,1,1024,128]{2,1,0,3:T(1,128)S(1)}, u32[]{:S(2)}, u32[]{:S(2)}) %all-to-all-start.3) | async-done | bytes 524320 | tf_op jit(solution)/shard_map/all_to_all | solution.py:135
  43.1 4.1 all-to-all-start
  62.1 3.9 collective-permute-done.8
  65.9 5.2 collective-permute-start.13
  71.2 11.0 %collective-permute-start.14 = (f32[2,2,1,1024,16]{3,4,1,0,2:T(8,128)S(1)}, f32[2,2,1,1024,16]{3,4,1,0,2:T(8,128)S(1)}, u32[]{:S(2)}, u32[]{:S(2)}) collective-permute-start(f32[2,2,1,1024,16]{3,4,1,0,2:T(8,128)S(1)} %bitcast.502), channel_id=1, source_target_pairs={{0,28},{4,24},{8,20},{12,16},{16,12},{20,8},{24,4},{28,0},{1,29},{... | collective-permute-start | bytes 786440 | tf_op jit(solution)/shard_map/ppermute | solution.py:28
  85.1 17.3 %collective-permute-done.11 = f32[2,2,1,1024,16]{3,4,1,0,2:T(8,128)S(1)} collective-permute-done((f32[2,2,1,1024,16]{3,4,1,0,2:T(8,128)S(1)}, f32[2,2,1,1024,16]{3,4,1,0,2:T(8,128)S(1)}, u32[]{:S(2)}, u32[]{:S(2)}) %collective-permute-start.11) | collective-permute-done | bytes 262176 | tf_op jit(solution)/shard_map/ppermute | solution.py:28
  102.5 6.1 collective-permute-done.12
  113.6 4.1 fusion.60
  117.7 4.2 fusion.34
  121.9 4.2 fusion.64
  126.2 5.4 subtract_bitcast_fusion.1
  142.5 4.4 fusion.73
  150.6 10.4 %collective-permute-start.2 = (f32[2,2,2,1024,16]{3,4,2,1,0:T(8,128)S(1)}, f32[2,2,2,1024,16]{3,4,2,1,0:T(8,128)S(1)}, u32[]{:S(2)}, u32[]{:S(2)}) collective-permute-start(f32[2,2,2,1024,16]{3,4,2,1,0:T(8,128)S(1)} %bitcast.494), channel_id=1, source_target_pairs={{0,8},{4,12},{8,0},{12,4},{16,24},{20,28},{24,16},{28,20},{1,9},{5... | collective-permute-start | bytes 1572872 | tf_op jit(solution)/shard_map/ppermute | solution.py:28
  170.0 22.5 %collective-permute-done.2 = f32[2,2,2,1024,16]{3,4,2,1,0:T(8,128)S(1)} collective-permute-done((f32[2,2,2,1024,16]{3,4,2,1,0:T(8,128)S(1)}, f32[2,2,2,1024,16]{3,4,2,1,0:T(8,128)S(1)}, u32[]{:S(2)}, u32[]{:S(2)}) %collective-permute-start.2) | collective-permute-done | bytes 524320 | tf_op jit(solution)/shard_map/ppermute | solution.py:28
  195.7 8.1 %collective-permute-done.3 = f32[2,2,2,1024,16]{3,4,2,1,0:T(8,128)S(1)} collective-permute-done((f32[2,2,2,1024,16]{3,4,2,1,0:T(8,128)S(1)}, f32[2,2,2,1024,16]{3,4,2,1,0:T(8,128)S(1)}, u32[]{:S(2)}, u32[]{:S(2)}) %collective-permute-start.3) | collective-permute-done | bytes 524320 | tf_op jit(solution)/shard_map/ppermute | solution.py:28
  205.5 30.8 %collective-permute-done.5 = f32[2,2,2,1024,16]{3,4,2,1,0:T(8,128)S(1)} collective-permute-done((f32[2,2,2,1024,16]{3,4,2,1,0:T(8,128)S(1)}, f32[2,2,2,1024,16]{3,4,2,1,0:T(8,128)S(1)}, u32[]{:S(2)}, u32[]{:S(2)}) %collective-permute-start.5) | collective-permute-done | bytes 524320 | tf_op jit(solution)/shard_map/ppermute | solution.py:28
  238.8 5.1 gather_fusion
  247.8 7.9 %fusion.26 = f32[2,2,1024,64,2]{2,4,3,1,0:T(2,128)S(1)} fusion(f32[2,2,1024,2,64]{2,4,3,1,0:T(8,128)S(1)} %get-tuple-element.77), kind=kOutput, calls=%fused_computation.80 | convolution fusion | flops 12582968 | bytes 4194304 | tf_op jit(solution)/shard_map/cb,...ba->...ca/dot_general | solution.py:54
  255.7 8.0 %fusion.22 = f32[2,2,1024,64,2]{2,4,3,1,0:T(2,128)S(1)} fusion(f32[2,2,1024,2,64]{2,4,3,1,0:T(8,128)S(1)} %get-tuple-element.78), kind=kOutput, calls=%fused_computation.76 | convolution fusion | flops 12582968 | bytes 4194304 | tf_op jit(solution)/shard_map/cb,...ba->...ca/dot_general | solution.py:54
  263.7 8.2 %convolution_add_fusion = f32[2,2,1024,64,2]{2,4,3,1,0:T(2,128)S(1)} fusion(f32[2,2,1024,64,2]{2,4,3,1,0:T(2,128)S(1)} %fusion.26, f32[2,2,1024,2,64]{2,4,3,1,0:T(8,128)S(1)} %get-tuple-element.78), kind=kOutput, calls=%fused_computation.73 | convolution fusion | flops 13107256 | bytes 6291456 | tf_op jit(solution)/shard_map/cb,...ba->...ca/dot_general | solution.py:54
  272.0 10.8 %fusion.2 = (f32[2,2,1024,2,64]{2,3,4,1,0:T(2,128)S(1)}, f32[2,2,1024,2,64]{2,3,4,1,0:T(2,128)S(1)}) fusion(f32[2,2,1024,64,2]{2,4,3,1,0:T(2,128)S(1)} %convolution_add_fusion, f32[2,64]{0,1:T(8,128)S(1)} %copy-done.35, f32[2,64]{0,1:T(8,128)S(1)} %copy.290, f32[2,2,1024,64,2]{2,4,3,1,0:T(2,128)S(1)} %fusion.22, ...), kind=kOutput, calls=%fused_computation.46 | convolution fusion | flops 16252984 | bytes 10486784 | tf_op jit(solution)/shard_map/cb,...ba->...ca/dot_general | solution.py:54
  306.8 9.4 %multiply_subtract_fusion = (f32[2,2,1024,2,64]{2,3,4,1,0:T(2,128)S(1)}, f32[2,2,1024,2,64]{2,3,4,1,0:T(2,128)S(1)}) fusion(f32[2,64]{0,1:T(8,128)S(1)} %copy-done.35, f32[2,64]{0,1:T(8,128)S(1)} %copy.290, f32[2,2,1024,2,64]{2,4,3,1,0:T(8,128)S(1)} %fusion.13, f32[2,2,1024,2,64]{2,4,3,1,0:T(8,128)S(1)} %fusion.15, f32[2,2,1024,2,64]{2,4,3,1,0:T(8,128)S(1)} %fusion.14, ...), kind=kLoop, calls=%fused_computation.55 | loop fusion | flops 4194304 | bytes 12583936 | tf_op jit(solution)/shard_map/sub | solution.py:62
  316.2 7.5 %fusion.248 = f32[2,2,1024,64,2]{2,4,3,1,0:T(2,128)S(1)} fusion(f32[2,2,1024,2,64]{2,3,4,1,0:T(2,128)S(1)} %get-tuple-element.69), kind=kOutput, calls=%fused_computation.407 | convolution fusion | flops 12582968 | bytes 4194304 | tf_op jit(solution)/shard_map/bc,...ca->...ba/dot_general | solution.py:54
  323.8 7.5 %fusion.246 = f32[2,2,1024,64,2]{2,4,3,1,0:T(2,128)S(1)} fusion(f32[2,2,1024,2,64]{2,3,4,1,0:T(2,128)S(1)} %get-tuple-element.70), kind=kOutput, calls=%fused_computation.405 | convolution fusion | flops 12582968 | bytes 4194304 | tf_op jit(solution)/shard_map/bc,...ca->...ba/dot_general | solution.py:54
  331.3 8.4 %subtract_bitcast_fusion = f32[2,2,1024,2,64]{2,3,4,1,0:T(2,128)S(1)} fusion(f32[2,2,1024,64,2]{2,4,3,1,0:T(2,128)S(1)} %fusion.248, f32[2,2,1024,2,64]{2,3,4,1,0:T(2,128)S(1)} %get-tuple-element.70), kind=kOutput, calls=%fused_computation.53 | convolution fusion | flops 13107256 | bytes 6291456 | tf_op jit(solution)/shard_map/bc,...ca->...ba/dot_general | solution.py:54
  340.3 8.0 %add_bitcast_fusion = f32[2,2,1024,2,64]{2,3,4,1,0:T(2,128)S(1)} fusion(f32[2,2,1024,64,2]{2,4,3,1,0:T(2,128)S(1)} %fusion.246, f32[2,2,1024,2,64]{2,3,4,1,0:T(2,128)S(1)} %get-tuple-element.69), kind=kOutput, calls=%fused_computation.52 | convolution fusion | flops 13107256 | bytes 6291456 | tf_op jit(solution)/shard_map/bc,...ca->...ba/dot_general | solution.py:54
  350.5 5.3 copy.332
  355.8 22.2 %all-to-all-start.4 = ((f32[2,2,2,1024,128]{3,2,1,0,4:T(2,128)}), f32[2,2,2,1024,128]{3,2,1,0,4:T(2,128)}, u32[]{:S(2)}, u32[]{:S(2)}) async-start(f32[2,2,2,1024,128]{3,2,1,0,4:T(2,128)} %copy.332), calls=%async_computation.4 | async-start | bytes 8388608 | tf_op jit(solution)/shard_map/all_to_all | solution.py:170
  383.3 4.1 fusion.70
  387.4 4.3 fusion.37
  392.0 4.1 fusion.66
  396.1 4.7 fusion.36
  404.6 65.3 %all-to-all-done.4 = f32[2,2,2,1024,128]{3,2,1,0,4:T(2,128)} async-done(((f32[2,2,2,1024,128]{3,2,1,0,4:T(2,128)}), f32[2,2,2,1024,128]{3,2,1,0,4:T(2,128)}, u32[]{:S(2)}, u32[]{:S(2)}) %all-to-all-start.4) | async-done | bytes 4194336 | tf_op jit(solution)/shard_map/all_to_all | solution.py:170
  469.9 3.6 all-to-all-start.1
  473.6 4.6 copy.333
  483.0 3.7 squeeze.120
  486.6 4.5 copy.335
  491.1 3.7 squeeze.121
  500.5 21.6 %all-to-all-done.1 = f32[2,2,1,1024,128]{3,1,2,0,4:T(2,128)S(1)} async-done(((f32[2,2,1,1024,128]{3,1,2,0,4:T(2,128)}), f32[2,2,1,1024,128]{3,1,2,0,4:T(2,128)S(1)}, u32[]{:S(2)}, u32[]{:S(2)}) %all-to-all-start.1) | async-done | bytes 2097184 | tf_op jit(solution)/shard_map/all_to_all | solution.py:170
  522.0 4.4 all-to-all-start.5
  535.5 16.5 %all-to-all-done.5 = f32[8,2,1024,16]{2,3,1,0:T(8,128)} async-done(((f32[8,2,1024,16]{2,3,1,0:T(8,128)}), f32[8,2,1024,16]{2,3,1,0:T(8,128)}, u32[]{:S(2)}, u32[]{:S(2)}) %all-to-all-start.5) | async-done | bytes 1048608 | tf_op jit(solution)/shard_map/all_to_all | solution.py:183
  552.1 4.1 all-to-all-start.2
  558.8 11.5 %all-to-all-done.2 = f32[8,1,1024,16]{2,3,1,0:T(8,128)} async-done(((f32[8,1,1024,16]{2,3,1,0:T(8,128)}), f32[8,1,1024,16]{2,3,1,0:T(8,128)}, u32[]{:S(2)}, u32[]{:S(2)}) %all-to-all-start.2) | async-done | bytes 524320 | tf_op jit(solution)/shard_map/all_to_all | solution.py:183
  573.9 35.7 %all-reduce = (f32[3,3,1024]{2,0,1:T(4,128)S(1)}, f32[1024]{0:T(1024)S(1)}, f32[1024]{0:T(1024)S(1)}) all-reduce(f32[3,3,1024]{2,0,1:T(4,128)S(1)} %pad_maximum_fusion.12, f32[1024]{0:T(1024)S(1)} %get-tuple-element.131, f32[1024]{0:T(1024)S(1)} %get-tuple-element.121), channel_id=1, replica_groups=mesh['ctx'=8,'chan'=4] {'ctx'}, use_global_device_ids=true, to_apply=%region_3.4 | all-reduce | flops 11264 | bytes 90112 | tf_op jit(solution)/shard_map/psum | solution.py:265
  613.5 39.2 %psum.36 = f32[64,64]{1,0:T(8,128)S(1)} all-reduce(f32[64,64]{1,0:T(8,128)S(1)} %fusion.120), channel_id=1, replica_groups=mesh['ctx'=8,'chan'=4] {'ctx','chan'}, use_global_device_ids=true, to_apply=%region_4.5 | all-reduce | flops 4096 | bytes 32768 | tf_op jit(solution)/shard_map/psum | solution.py:268
  663.1 66.1 %all-reduce.3.cloned.1.call-done = f32[64,1024]{1,0:T(8,128)} async-done(((f32[64,1024]{1,0:T(8,128)}), f32[64,1024]{1,0:T(8,128)}) %all-reduce.3.cloned.1.call-update) | async-done | bytes 262160 | tf_op jit(solution)/shard_map/psum | solution.py:265
  (283 shorter events, 150.7 us)
Async XLA Ops:
  7.2 22.6 %copy-start = (f32[64,1024]{1,0:T(8,128)S(1)}, f32[64,1024]{1,0:T(8,128)}, u32[]{:S(2)}) copy-start(f32[64,1024]{1,0:T(8,128)} %param.14) | copy-start | bytes 786436
  8.3 7.6 %copy-start.40 = (f32[3,3,1024]{2,1,0:T(4,128)S(1)}, f32[3,3,1024]{2,1,0:T(4,128)}, u32[]{:S(2)}) copy-start(f32[3,3,1024]{2,1,0:T(4,128)} %param.12) | copy-start | bytes 110596
  9.5 11.0 %copy-start.14 = (bf16[1024,128]{0,1:T(8,128)(2,1)}, bf16[1024,128]{0,1:T(8,128)(2,1)S(1)}, u32[]{:S(2)}) copy-start(bf16[1024,128]{0,1:T(8,128)(2,1)S(1)} %copy.279) | copy-start | bytes 786436
  9.6 9.3 %copy-start.49 = (f32[1024]{0:T(1024)S(1)}, f32[1024]{0:T(1024)}, u32[]{:S(2)}) copy-start(f32[1024]{0:T(1024)} %param.15) | copy-start | bytes 12292
  9.6 10.1 %copy-start.24 = (bf16[1024,128]{1,0:T(8,128)(2,1)S(1)}, bf16[1024,128]{1,0:T(8,128)(2,1)}, u32[]{:S(2)}) copy-start(bf16[1024,128]{1,0:T(8,128)(2,1)} %param.17) | copy-start | bytes 786436
  10.8 9.8 %copy-start.16 = (bf16[1024,128]{0,1:T(8,128)(2,1)}, bf16[1024,128]{0,1:T(8,128)(2,1)S(1)}, u32[]{:S(2)}) copy-start(bf16[1024,128]{0,1:T(8,128)(2,1)S(1)} %copy.280) | copy-start | bytes 786436
  11.0 11.4 %copy-start.2 = (f32[3,1024,128]{1,2,0:T(8,128)}, f32[3,1024,128]{1,2,0:T(8,128)S(1)}, u32[]{:S(2)}) copy-start(f32[3,1024,128]{1,2,0:T(8,128)S(1)} %get-tuple-element.129) | copy-start | bytes 4718596
  11.0 9.5 %collective-permute-start = (bf16[3,1024,2]{1,2,0:T(2,128)(2,1)S(1)}, bf16[3,1024,2]{1,2,0:T(2,128)(2,1)S(1)}, u32[]{:S(2)}, u32[]{:S(2)}) collective-permute-start(bf16[3,1024,2]{1,2,0:T(2,128)(2,1)S(1)} %slice.143), channel_id=1, source_target_pairs={{0,4},{4,8},{8,12},{12,16},{16,20},{20,24},{24,28},{1,5},{5,9},{9,... | collective-permute-start | bytes 36872 | tf_op jit(solution)/shard_map/ppermute | solution.py:36
  15.9 4.7 copy-start.42
  15.9 4.7 copy-start.44
  18.1 4.4 copy-start.25
  18.2 10.6 %copy-start.31 = (f32[32,128]{1,0:T(8,128)}, f32[32,128]{1,0:T(8,128)S(1)}, u32[]{:S(2)}) copy-start(f32[32,128]{1,0:T(8,128)S(1)} %get-tuple-element.137) | copy-start | bytes 49156
  18.2 10.6 %copy-start.33 = (f32[32,128]{1,0:T(8,128)}, f32[32,128]{1,0:T(8,128)S(1)}, u32[]{:S(2)}) copy-start(f32[32,128]{1,0:T(8,128)S(1)} %get-tuple-element.138) | copy-start | bytes 49156
  22.5 8.0 %copy-start.4 = (f32[3,1024,128]{1,2,0:T(8,128)}, f32[3,1024,128]{1,2,0:T(8,128)S(1)}, u32[]{:S(2)}) copy-start(f32[3,1024,128]{1,2,0:T(8,128)S(1)} %multiply_add_fusion.2) | copy-start | bytes 4718596
  22.6 6.3 copy-start.39
  22.6 7.2 copy-start.52
  23.9 19.1 %all-to-all-start.3 = ((f32[1,1,1024,128]{2,1,0,3:T(1,128)}), f32[1,1,1024,128]{2,1,0,3:T(1,128)S(1)}, u32[]{:S(2)}, u32[]{:S(2)}) async-start(f32[1,1,1024,128]{2,1,0,3:T(1,128)} %copy.310), calls=%async_computation.3 | async-start | bytes 1048576 | tf_op jit(solution)/shard_map/all_to_all | solution.py:135
  28.8 19.7 %copy-start.50 = (s32[8,2]{0,1:T(2,128)}, s32[8,2]{0,1:T(2,128)S(1)}, u32[]{:S(2)}) copy-start(s32[8,2]{0,1:T(2,128)S(1)} %multiply_add_fusion.9) | copy-start | bytes 196
  43.1 92.5 %all-to-all-start = ((f32[1,2,1024,128]{2,1,0,3:T(2,128)}), f32[1,2,1024,128]{2,1,0,3:T(2,128)S(1)}, u32[]{:S(2)}, u32[]{:S(2)}) async-start(f32[1,2,1024,128]{2,1,0,3:T(2,128)} %copy.281), calls=%async_computation | async-start | bytes 2097152 | tf_op jit(solution)/shard_map/all_to_all | solution.py:135
  52.9 13.0 %collective-permute-start.8 = (f32[2,2,1,1024,16]{3,4,1,0,2:T(8,128)S(1)}, f32[2,2,1,1024,16]{3,4,1,0,2:T(8,128)S(1)}, u32[]{:S(2)}, u32[]{:S(2)}) collective-permute-start(f32[2,2,1,1024,16]{3,4,1,0,2:T(8,128)S(1)} %bitcast.506), channel_id=1, source_target_pairs={{0,4},{4,0},{8,12},{12,8},{16,20},{20,16},{24,28},{28,24},{1,5},{5... | collective-permute-start | bytes 786440 | tf_op jit(solution)/shard_map/ppermute | solution.py:28
  55.1 16.1 %collective-permute-start.9 = (f32[2,2,1,1024,16]{3,4,1,0,2:T(8,128)S(1)}, f32[2,2,1,1024,16]{3,4,1,0,2:T(8,128)S(1)}, u32[]{:S(2)}, u32[]{:S(2)}) collective-permute-start(f32[2,2,1,1024,16]{3,4,1,0,2:T(8,128)S(1)} %bitcast.503), channel_id=1, source_target_pairs={{0,8},{4,12},{8,0},{12,4},{16,24},{20,28},{24,16},{28,20},{1,9},{5... | collective-permute-start | bytes 786440 | tf_op jit(solution)/shard_map/ppermute | solution.py:28
  56.7 28.4 %collective-permute-start.10 = (f32[2,2,1,1024,16]{3,4,1,0,2:T(8,128)S(1)}, f32[2,2,1,1024,16]{3,4,1,0,2:T(8,128)S(1)}, u32[]{:S(2)}, u32[]{:S(2)}) collective-permute-start(f32[2,2,1,1024,16]{3,4,1,0,2:T(8,128)S(1)} %bitcast.501), channel_id=1, source_target_pairs={{0,12},{4,8},{8,4},{12,0},{16,28},{20,24},{24,20},{28,16},{1,13},{... | collective-permute-start | bytes 786440 | tf_op jit(solution)/shard_map/ppermute | solution.py:28
  56.8 45.7 %collective-permute-start.11 = (f32[2,2,1,1024,16]{3,4,1,0,2:T(8,128)S(1)}, f32[2,2,1,1024,16]{3,4,1,0,2:T(8,128)S(1)}, u32[]{:S(2)}, u32[]{:S(2)}) collective-permute-start(f32[2,2,1,1024,16]{3,4,1,0,2:T(8,128)S(1)} %bitcast.500), channel_id=1, source_target_pairs={{0,16},{4,20},{8,24},{12,28},{16,0},{20,4},{24,8},{28,12},{1,17},{... | collective-permute-start | bytes 786440 | tf_op jit(solution)/shard_map/ppermute | solution.py:28
  60.4 48.1 %collective-permute-start.12 = (f32[2,2,1,1024,16]{3,4,1,0,2:T(8,128)S(1)}, f32[2,2,1,1024,16]{3,4,1,0,2:T(8,128)S(1)}, u32[]{:S(2)}, u32[]{:S(2)}) collective-permute-start(f32[2,2,1,1024,16]{3,4,1,0,2:T(8,128)S(1)} %bitcast.504), channel_id=1, source_target_pairs={{0,20},{4,16},{8,28},{12,24},{16,4},{20,0},{24,12},{28,8},{1,21},{... | collective-permute-start | bytes 786440 | tf_op jit(solution)/shard_map/ppermute | solution.py:28
  65.9 42.7 %collective-permute-start.13 = (f32[2,2,1,1024,16]{3,4,1,0,2:T(8,128)S(1)}, f32[2,2,1,1024,16]{3,4,1,0,2:T(8,128)S(1)}, u32[]{:S(2)}, u32[]{:S(2)}) collective-permute-start(f32[2,2,1,1024,16]{3,4,1,0,2:T(8,128)S(1)} %bitcast.505), channel_id=1, source_target_pairs={{0,24},{4,28},{8,16},{12,20},{16,8},{20,12},{24,0},{28,4},{1,25},{... | collective-permute-start | bytes 786440 | tf_op jit(solution)/shard_map/ppermute | solution.py:28
  71.2 37.4 %collective-permute-start.14 = (f32[2,2,1,1024,16]{3,4,1,0,2:T(8,128)S(1)}, f32[2,2,1,1024,16]{3,4,1,0,2:T(8,128)S(1)}, u32[]{:S(2)}, u32[]{:S(2)}) collective-permute-start(f32[2,2,1,1024,16]{3,4,1,0,2:T(8,128)S(1)} %bitcast.502), channel_id=1, source_target_pairs={{0,28},{4,24},{8,20},{12,16},{16,12},{20,8},{24,4},{28,0},{1,29},{... | collective-permute-start | bytes 786440 | tf_op jit(solution)/shard_map/ppermute | solution.py:28
  147.0 20.6 %collective-permute-start.1 = (f32[2,2,2,1024,16]{3,4,2,1,0:T(8,128)S(1)}, f32[2,2,2,1024,16]{3,4,2,1,0:T(8,128)S(1)}, u32[]{:S(2)}, u32[]{:S(2)}) collective-permute-start(f32[2,2,2,1024,16]{3,4,2,1,0:T(8,128)S(1)} %bitcast.495), channel_id=1, source_target_pairs={{0,4},{4,0},{8,12},{12,8},{16,20},{20,16},{24,28},{28,24},{1,5},{5... | collective-permute-start | bytes 1572872 | tf_op jit(solution)/shard_map/ppermute | solution.py:28
  150.6 41.8 %collective-permute-start.2 = (f32[2,2,2,1024,16]{3,4,2,1,0:T(8,128)S(1)}, f32[2,2,2,1024,16]{3,4,2,1,0:T(8,128)S(1)}, u32[]{:S(2)}, u32[]{:S(2)}) collective-permute-start(f32[2,2,2,1024,16]{3,4,2,1,0:T(8,128)S(1)} %bitcast.494), channel_id=1, source_target_pairs={{0,8},{4,12},{8,0},{12,4},{16,24},{20,28},{24,16},{28,20},{1,9},{5... | collective-permute-start | bytes 1572872 | tf_op jit(solution)/shard_map/ppermute | solution.py:28
  162.3 41.5 %collective-permute-start.3 = (f32[2,2,2,1024,16]{3,4,2,1,0:T(8,128)S(1)}, f32[2,2,2,1024,16]{3,4,2,1,0:T(8,128)S(1)}, u32[]{:S(2)}, u32[]{:S(2)}) collective-permute-start(f32[2,2,2,1024,16]{3,4,2,1,0:T(8,128)S(1)} %bitcast.496), channel_id=1, source_target_pairs={{0,12},{4,8},{8,4},{12,0},{16,28},{20,24},{24,20},{28,16},{1,13},{... | collective-permute-start | bytes 1572872 | tf_op jit(solution)/shard_map/ppermute | solution.py:28
  164.2 40.4 %collective-permute-start.4 = (f32[2,2,2,1024,16]{3,4,2,1,0:T(8,128)S(1)}, f32[2,2,2,1024,16]{3,4,2,1,0:T(8,128)S(1)}, u32[]{:S(2)}, u32[]{:S(2)}) collective-permute-start(f32[2,2,2,1024,16]{3,4,2,1,0:T(8,128)S(1)} %bitcast.499), channel_id=1, source_target_pairs={{0,16},{4,20},{8,24},{12,28},{16,0},{20,4},{24,8},{28,12},{1,17},{... | collective-permute-start | bytes 1572872 | tf_op jit(solution)/shard_map/ppermute | solution.py:28
  166.4 69.9 %collective-permute-start.5 = (f32[2,2,2,1024,16]{3,4,2,1,0:T(8,128)S(1)}, f32[2,2,2,1024,16]{3,4,2,1,0:T(8,128)S(1)}, u32[]{:S(2)}, u32[]{:S(2)}) collective-permute-start(f32[2,2,2,1024,16]{3,4,2,1,0:T(8,128)S(1)} %bitcast.497), channel_id=1, source_target_pairs={{0,20},{4,16},{8,28},{12,24},{16,4},{20,0},{24,12},{28,8},{1,21},{... | collective-permute-start | bytes 1572872 | tf_op jit(solution)/shard_map/ppermute | solution.py:28
  167.6 69.5 %collective-permute-start.6 = (f32[2,2,2,1024,16]{3,4,2,1,0:T(8,128)S(1)}, f32[2,2,2,1024,16]{3,4,2,1,0:T(8,128)S(1)}, u32[]{:S(2)}, u32[]{:S(2)}) collective-permute-start(f32[2,2,2,1024,16]{3,4,2,1,0:T(8,128)S(1)} %bitcast.498), channel_id=1, source_target_pairs={{0,24},{4,28},{8,16},{12,20},{16,8},{20,12},{24,0},{28,4},{1,25},{... | collective-permute-start | bytes 1572872 | tf_op jit(solution)/shard_map/ppermute | solution.py:28
  192.5 45.5 %collective-permute-start.7 = (f32[2,2,2,1024,16]{3,4,2,1,0:T(8,128)S(1)}, f32[2,2,2,1024,16]{3,4,2,1,0:T(8,128)S(1)}, u32[]{:S(2)}, u32[]{:S(2)}) collective-permute-start(f32[2,2,2,1024,16]{3,4,2,1,0:T(8,128)S(1)} %bitcast.493), channel_id=1, source_target_pairs={{0,28},{4,24},{8,20},{12,16},{16,12},{20,8},{24,4},{28,0},{1,29},{... | collective-permute-start | bytes 1572872 | tf_op jit(solution)/shard_map/ppermute | solution.py:28
  355.8 114.1 %all-to-all-start.4 = ((f32[2,2,2,1024,128]{3,2,1,0,4:T(2,128)}), f32[2,2,2,1024,128]{3,2,1,0,4:T(2,128)}, u32[]{:S(2)}, u32[]{:S(2)}) async-start(f32[2,2,2,1024,128]{3,2,1,0,4:T(2,128)} %copy.332), calls=%async_computation.4 | async-start | bytes 8388608 | tf_op jit(solution)/shard_map/all_to_all | solution.py:170
  469.9 52.1 %all-to-all-start.1 = ((f32[2,2,1,1024,128]{3,1,2,0,4:T(2,128)}), f32[2,2,1,1024,128]{3,1,2,0,4:T(2,128)S(1)}, u32[]{:S(2)}, u32[]{:S(2)}) async-start(f32[2,2,1,1024,128]{3,1,2,0,4:T(2,128)} %copy.304), calls=%async_computation.1 | async-start | bytes 4194304 | tf_op jit(solution)/shard_map/all_to_all | solution.py:170
  522.0 30.0 %all-to-all-start.5 = ((f32[8,2,1024,16]{2,3,1,0:T(8,128)}), f32[8,2,1024,16]{2,3,1,0:T(8,128)}, u32[]{:S(2)}, u32[]{:S(2)}) async-start(f32[8,2,1024,16]{2,3,1,0:T(8,128)} %copy.336), calls=%async_computation.5 | async-start | bytes 2097152 | tf_op jit(solution)/shard_map/all_to_all | solution.py:183
  534.4 24.1 %copy-start.11 = (f32[1024,128]{0,1:T(8,128)S(1)}, f32[1024,128]{0,1:T(8,128)}, u32[]{:S(2)}) copy-start(f32[1024,128]{0,1:T(8,128)} %copy-done.10) | copy-start | bytes 1572868
  534.4 24.1 %copy-start.53 = (f32[128]{0:T(128)S(1)}, f32[128]{0:T(128)}, u32[]{:S(2)}) copy-start(f32[128]{0:T(128)} %get-tuple-element.147) | copy-start | bytes 1540
  534.4 24.1 %copy-start.54 = (f32[128]{0:T(128)S(1)}, f32[128]{0:T(128)}, u32[]{:S(2)}) copy-start(f32[128]{0:T(128)} %get-tuple-element.148) | copy-start | bytes 1540
  552.1 18.2 %all-to-all-start.2 = ((f32[8,1,1024,16]{2,3,1,0:T(8,128)}), f32[8,1,1024,16]{2,3,1,0:T(8,128)}, u32[]{:S(2)}, u32[]{:S(2)}) async-start(f32[8,1,1024,16]{2,3,1,0:T(8,128)} %copy.308), calls=%async_computation.2 | async-start | bytes 1048576 | tf_op jit(solution)/shard_map/all_to_all | solution.py:183
  556.2 14.1 %copy-start.5 = (f32[3,1024,128]{1,2,0:T(8,128)S(1)}, f32[3,1024,128]{1,2,0:T(8,128)}, u32[]{:S(2)}) copy-start(f32[3,1024,128]{1,2,0:T(8,128)} %copy-done.4) | copy-start | bytes 4718596
  556.2 14.1 %copy-start.23 = (bf16[1024,128]{0,1:T(8,128)(2,1)S(1)}, bf16[1024,128]{0,1:T(8,128)(2,1)}, u32[]{:S(2)}) copy-start(bf16[1024,128]{0,1:T(8,128)(2,1)} %copy.309) | copy-start | bytes 786436
  556.2 14.1 %copy-start.48 = (f32[1024]{0:T(1024)S(1)}, f32[1024]{0:T(1024)}, u32[]{:S(2)}) copy-start(f32[1024]{0:T(1024)} %param.16) | copy-start | bytes 12292
  556.2 172.9 %all-reduce.3.cloned.1.call-start = ((), (), s32[]{:S(2)}) async-start(), calls=%async_computation.6 | async-start | bytes 524288 | tf_op jit(solution)/shard_map/psum | solution.py:265
  572.8 39.9 %copy-start.36 = (f32[128,64]{0,1:T(8,128)S(1)}, f32[128,64]{0,1:T(8,128)}, u32[]{:S(2)}) copy-start(f32[128,64]{0,1:T(8,128)} %get-tuple-element.142) | copy-start | bytes 98308
  572.8 40.5 %copy-start.32 = (f32[32,128]{1,0:T(8,128)S(1)}, f32[32,128]{1,0:T(8,128)}, u32[]{:S(2)}) copy-start(f32[32,128]{1,0:T(8,128)} %copy-done.31) | copy-start | bytes 49156
  572.8 40.5 %copy-start.34 = (f32[32,128]{1,0:T(8,128)S(1)}, f32[32,128]{1,0:T(8,128)}, u32[]{:S(2)}) copy-start(f32[32,128]{1,0:T(8,128)} %copy-done.33) | copy-start | bytes 49156
  610.2 47.8 %collective-permute-start.15 = (f32[3,1024,2]{1,2,0:T(2,128)S(1)}, f32[3,1024,2]{1,2,0:T(2,128)S(1)}, u32[]{:S(2)}, u32[]{:S(2)}) collective-permute-start(f32[3,1024,2]{1,2,0:T(2,128)S(1)} %slice.165), channel_id=1, source_target_pairs={{4,0},{8,4},{12,8},{16,12},{20,16},{24,20},{28,24},{5,1},{9,5},{13... | collective-permute-start | bytes 73736 | tf_op jit(solution)/shard_map/ppermute | solution.py:36
  (30 other events, 69.7 us)
Sparse Core Ops, SparseCore 0:
  658.1 70.9 all-reduce.2
